TPU v7x, 512 devices: a whole 4x4x16 slice. The times are simulated.
512 devices in a mesh: dp: 16 (over z), tensor: 32 (over x, y, core).
Axes of the slice: x: 4, y: 4, z: 16, core: 2. Of those that a mesh axis runs over, the one named last changes fastest.
Arguments:
- pages: bfloat16 [2, 64, 64, 2048], P(None, 'dp', None, 'tensor'), may hold values from -8 to 8
- page_table: int32 [16, 2], replicated, may hold values from 0 to 63, as said below
- page_count: int32 [16], replicated, may hold values from 1 to 2
- last_len: int32 [16], replicated, may hold values from 1 to 64
- targets: int32 [16, 128], P('dp'), may hold values from 0 to 65535
- mix_key: float32 [2, 2048], P(None, 'tensor'), may hold values from 0.05 to 0.95
- w_key: bfloat16 [2, 2048, 8192], P(None, None, 'tensor'), may hold values from -0.125 to 0.125
- w_value: bfloat16 [2, 8192, 2048], P(None, 'tensor'), may hold values from -0.0625 to 0.0625
- ln_gain: float32 [2, 2048], replicated, may hold values from 0.5 to 1.5
- ln_bias: float32 [2, 2048], replicated, may hold values from -2 to 2
- head: bfloat16 [2, 2048, 65536], P(None, 'dp', 'tensor'), may hold values from -8 to 8
Outputs:
- token_logprob: float32 [16, 128], P('dp', 'tensor')
- ratio_sum: float32 [16], P('dp')
Inputs may be any that keep to these rules, and one draw needn't show every extreme that they name: Entries are distinct; the page lives on dp device page_table[r, p] // 4.
All inputs are finite; a program needn't handle non-finite values.
Results may differ from a plain program's by a relative error of at most 0.0029.
The roundings to bfloat16 on the way count: a program that leaves them out, or rounds other values in their place, can miss the bound.
Values may be sent and summed in bfloat16 or wider, within the bound.
A program may use at most 128 MiB of HBM per device.

v0:
```python
import jax
import jax.numpy as jnp
from jax import lax
from jax.sharding import PartitionSpec as P

D = 2048
epsilon = 1e-05


def joined(value, axis, join):
    pieces = jax.tree.map(lambda part: lax.all_gather(part, axis), value)
    head = jax.tree.map(lambda part: part[0], pieces)
    tail = jax.tree.map(lambda part: part[1:], pieces)
    total, _ = lax.scan(lambda total, piece: (join(total, piece), None), head, tail)
    return total


def combine(left_stats, right_stats):
    peak = jnp.maximum(left_stats[0], right_stats[0])
    totals = left_stats[1] * jnp.exp(left_stats[0] - peak) + right_stats[1] * jnp.exp(
        right_stats[0] - peak
    )
    return (peak, totals, left_stats[2] + right_stats[2])


def body(
    pages,
    page_table,
    page_count,
    last_len,
    targets,
    mix_key,
    w_key,
    w_value,
    ln_gain,
    ln_bias,
    head,
):
    tensor_count = lax.axis_size("tensor")
    owner = lax.axis_index("dp")
    tensor_index = lax.axis_index("tensor")
    page_len = pages.shape[2]
    width_local = pages.shape[3]
    page_cap = page_table.shape[1]
    slot_count = page_cap * page_len
    live_pages = jnp.arange(page_cap)[None, :] < page_count[:, None]
    table_row = page_table[owner]
    everything = lax.all_gather(pages, "dp", axis=1, tiled=True)
    states = jnp.take(everything, table_row, axis=1)
    states = jnp.where(live_pages[owner][None, :, None, None], states, jnp.zeros_like(states))
    states = states.reshape(2, slot_count, width_local)
    state_f = states.astype(jnp.float32)
    previous = jnp.concatenate(
        [jnp.zeros((2, 1, width_local), jnp.float32), state_f[:, :-1]], axis=1
    )
    shifted = (state_f + (previous - state_f) * mix_key[:, None, :]).astype(jnp.bfloat16)
    hidden = jnp.einsum(
        "msd,mdf->msf",
        lax.all_gather(shifted, "tensor", axis=2, tiled=True),
        w_key,
        preferred_element_type=jnp.float32,
    )
    key_act = (jnp.maximum(hidden, 0.0) ** 2).astype(jnp.bfloat16)
    partial_out = jnp.einsum("msf,mfd->msd", key_act, w_value, preferred_element_type=jnp.float32)
    ffn_out = lax.psum_scatter(partial_out, "tensor", scatter_dimension=2, tiled=True)
    residual = state_f + ffn_out
    row_sum, row_square = lax.psum(
        (jnp.sum(residual, axis=-1), jnp.sum(residual * residual, axis=-1)), "tensor"
    )
    average = row_sum / D
    variance = row_square / D - average * average
    gain_local = lax.dynamic_slice_in_dim(ln_gain, tensor_index * width_local, width_local, 1)
    bias_local = lax.dynamic_slice_in_dim(ln_bias, tensor_index * width_local, width_local, 1)
    normed_local = (
        (residual - average[..., None])
        * lax.rsqrt(variance + epsilon)[..., None]
        * gain_local[:, None, :]
        + bias_local[:, None, :]
    ).astype(jnp.bfloat16)
    normed = lax.all_gather(normed_local, "tensor", axis=2, tiled=True)
    vocab_local = head.shape[2]
    logits = jnp.einsum(
        "msd,mdv->msv",
        normed,
        lax.all_gather(head, "dp", axis=1, tiled=True),
        preferred_element_type=jnp.float32,
    )
    peak = jnp.max(logits, axis=-1)
    totals = jnp.sum(jnp.exp(logits - peak[..., None]), axis=-1)
    vocab_ids = jnp.arange(vocab_local) + tensor_index * vocab_local
    matches = vocab_ids[None, None, :] == targets[0][None, :, None]
    target_logit = jnp.sum(jnp.where(matches, logits, 0.0), axis=-1)
    peak, totals, target_logit = joined((peak, totals, target_logit), "tensor", combine)
    logp = target_logit - peak - jnp.log(totals)
    length = (page_count[owner] - 1) * page_len + last_len[owner]
    valid = jnp.arange(slot_count) < length
    policy_row = jnp.where(valid, logp[0], 0.0)
    ratio = jnp.sum(jnp.where(valid, logp[0] - logp[1], 0.0))
    share = slot_count // tensor_count
    token_part = lax.dynamic_slice_in_dim(policy_row, tensor_index * share, share)[None, :]
    return (token_part, ratio[None])


def solution(mesh):
    placed = (
        P(None, "dp", None, "tensor"),
        P(),
        P(),
        P(),
        P("dp", None),
        P(None, "tensor"),
        P(None, None, "tensor"),
        P(None, "tensor", None),
        P(),
        P(),
        P(None, "dp", "tensor"),
    )
    return jax.shard_map(
        body, mesh=mesh, in_specs=placed, out_specs=(P("dp", "tensor"), P("dp")), check_vma=False
    )
```

profile of v0, /device:TPU:1, one launch (start us, length us, event | category | flops | bytes accessed | tf_op | source)
XLA Modules:
  0.0 654.3 jit_solution(647617080670465465)
XLA Ops:
  7.2 0.0 copy-start
  7.2 0.0 all-gather.11.cloned.1.call-start
  7.2 0.7 all-gather.11.cloned.1.call-update
  7.9 0.0 all-gather.13.cloned.1.call-start
  8.0 0.9 dynamic-slice_reduce_fusion
  8.8 1.2 dynamic_slice.31
  10.1 0.7 compare_bitcast_fusion
  10.7 0.1 broadcast_in_dim.65
  10.8 0.1 broadcast_in_dim.66
  10.9 0.1 broadcast_in_dim.68
  11.0 0.1 broadcast_in_dim.69
  11.1 68.5 %all-gather.11.cloned.1.call-done = bf16[2,64,64,64]{3,2,1,0:T(8,128)(2,1)} async-done(((bf16[2,4,64,64]{3,2,1,0:T(8,128)(2,1)}), bf16[2,64,64,64]{3,2,1,0:T(8,128)(2,1)}) %all-gather.11.cloned.1.call-update) | async-done | bytes 1048592 | tf_op jit(solution)/shard_map/all_gather | solution.py:48
  79.6 2.2 gather_fusion
  81.7 0.1 copy.15
  81.8 0.1 gather.7
  81.9 1.4 add_convert_fusion.1
  83.3 0.0 all-gather.13.cloned.1.call-update
  83.4 0.0 reduce-scatter.2.cloned.1.call-start
  83.4 64.8 %all-gather.13.cloned.1.call-done = bf16[2,128,2048]{1,2,0:T(8,128)(2,1)} async-done(((bf16[2,128,64]{1,2,0:T(8,128)(2,1)}), bf16[2,128,2048]{1,2,0:T(8,128)(2,1)}) %all-gather.13.cloned.1.call-update) | async-done | bytes 1048592 | tf_op jit(solution)/shard_map/all_gather | solution.py:59
  148.2 0.0 copy-done
  148.2 4.5 fusion.4
  152.7 0.0 copy-start.2
  152.7 0.0 copy-start.1
  152.7 0.0 reduce-scatter.2.cloned.1.call-update
  152.7 0.0 all-gather.15.cloned.1.call-start
  152.8 0.8 constant_dynamic-slice_fusion.1
  153.6 98.6 %reduce-scatter.2.cloned.1.call-done = f32[2,128,64]{1,2,0:T(8,128)} async-done(((f32[2,128,2048]{1,2,0:T(8,128)}), f32[2,128,64]{1,2,0:T(8,128)}) %reduce-scatter.2.cloned.1.call-update) | async-done | bytes 65552 | tf_op jit(solution)/shard_map/reduce_scatter | solution.py:65
  252.1 0.9 fusion.6
  253.0 64.3 %all-reduce.1 = (f32[2,128]{1,0:T(2,128)S(1)}, f32[2,128]{1,0:T(2,128)S(1)}) all-reduce(f32[2,128]{1,0:T(2,128)S(1)} %get-tuple-element.47, f32[2,128]{1,0:T(2,128)S(1)} %get-tuple-element.46), channel_id=1, replica_groups=mesh['dp'=16,'tensor'=32] {'tensor'}, use_global_device_ids=true, to_apply=%region_4.5 | all-reduce | flops 512 | bytes 4096 | tf_op jit(solution)/shard_map/psum | solution.py:67
  317.3 1.6 add_convert_fusion
  318.9 0.0 all-gather.15.cloned.1.call-update
  318.9 0.0 all-gather.17.cloned.1.call-start
  319.0 0.5 all-gather.17.cloned.1.call-update
  320.2 0.0 copy-done.2
  320.2 0.6 dynamic_slice.32
  321.4 0.0 copy-done.1
  321.4 0.2 broadcast_compare_fusion
  321.7 53.0 %all-gather.15.cloned.1.call-done = bf16[2,128,2048]{1,2,0:T(8,128)(2,1)} async-done(((bf16[2,128,64]{1,2,0:T(8,128)(2,1)}), bf16[2,128,2048]{1,2,0:T(8,128)(2,1)}) %all-gather.15.cloned.1.call-update) | async-done | bytes 1048592 | tf_op jit(solution)/shard_map/all_gather | solution.py:80
  374.6 191.1 %all-gather.17.cloned.1.call-done = bf16[2,2048,2048]{2,1,0:T(8,128)(2,1)} async-done(((bf16[2,128,2048]{2,1,0:T(8,128)(2,1)}), bf16[2,2048,2048]{2,1,0:T(8,128)(2,1)}) %all-gather.17.cloned.1.call-update) | async-done | bytes 16777232 | tf_op jit(solution)/shard_map/all_gather | solution.py:85
  565.7 8.6 %fusion.11 = (f32[2,128]{1,0:T(2,128)S(1)}, f32[2,128,2048]{2,1,0:T(8,128)S(1)}) fusion(bf16[2,128,2048]{1,2,0:T(8,128)(2,1)} %all-gather.15.cloned.1.call-done, bf16[2,2048,2048]{2,1,0:T(8,128)(2,1)} %all-gather.17.cloned.1.call-done), kind=kOutput, calls=%fused_computation.45 | convolution fusion | flops 2148007680 | bytes 19923968 | tf_op jit(solution)/shard_map/msd,mdv->msv/dot_general | solution.py:82
  574.4 0.7 select_reduce_fusion
  575.1 24.7 %all-gather.5 = f32[32,2,128]{2,1,0:T(2,128)S(1)} all-gather(f32[1,2,128]{2,1,0:T(2,128)S(1)} %bitcast.56), channel_id=4, replica_groups=mesh['dp'=16,'tensor'=32] {'tensor'}, dimensions={0}, use_global_device_ids=true | all-gather | bytes 33792 | tf_op jit(solution)/shard_map/all_gather | solution.py:11
  599.8 23.5 %all-gather.4 = f32[32,2,128]{2,1,0:T(2,128)S(1)} all-gather(f32[1,2,128]{2,1,0:T(2,128)S(1)} %bitcast.55), channel_id=3, replica_groups=mesh['dp'=16,'tensor'=32] {'tensor'}, dimensions={0}, use_global_device_ids=true | all-gather | bytes 33792 | tf_op jit(solution)/shard_map/all_gather | solution.py:11
  623.3 21.9 %all-gather.3 = f32[32,2,128]{2,1,0:T(2,128)S(1)} all-gather(f32[1,2,128]{2,1,0:T(2,128)S(1)} %bitcast.54), channel_id=2, replica_groups=mesh['dp'=16,'tensor'=32] {'tensor'}, dimensions={0}, use_global_device_ids=true | all-gather | bytes 33792 | tf_op jit(solution)/shard_map/all_gather | solution.py:11
  645.2 1.3 while.14
  646.5 0.6 fusion.7
  647.1 0.6 dynamic-slice_bitcast_fusion
  (44 shorter events, 1.0 us)
Async XLA Ops:
  7.2 141.0 %copy-start = (bf16[2,256,2048]{2,1,0:T(8,128)(2,1)S(1)}, bf16[2,256,2048]{2,1,0:T(8,128)(2,1)}, u32[]{:S(2)}) copy-start(bf16[2,256,2048]{2,1,0:T(8,128)(2,1)} %param.20) | copy-start | bytes 6291460
  7.2 72.4 %all-gather.11.cloned.1.call-start = ((), (), s32[]{:S(2)}) async-start(), calls=%async_computation.1 | async-start | bytes 2228224 | tf_op jit(solution)/shard_map/all_gather | solution.py:48
  7.9 140.3 %all-gather.13.cloned.1.call-start = ((), (), s32[]{:S(2)}) async-start(), calls=%async_computation.2 | async-start | bytes 1081344 | tf_op jit(solution)/shard_map/all_gather | solution.py:59
  83.4 168.8 %reduce-scatter.2.cloned.1.call-start = ((), (), s32[]{:S(2)}) async-start(), calls=%async_computation.3 | async-start | bytes 2162688 | tf_op jit(solution)/shard_map/reduce_scatter | solution.py:65
  152.7 167.5 %copy-start.2 = (s32[16]{0:T(128)S(1)}, s32[16]{0:T(128)}, u32[]{:S(2)}) copy-start(s32[16]{0:T(128)} %param.16) | copy-start | bytes 196
  152.7 168.7 %copy-start.1 = (s32[1,128]{1,0:T(1,128)S(1)}, s32[1,128]{1,0:T(1,128)}, u32[]{:S(2)}) copy-start(s32[1,128]{1,0:T(1,128)} %param.17) | copy-start | bytes 1540
  152.7 221.9 %all-gather.15.cloned.1.call-start = ((), (), s32[]{:S(2)}) async-start(), calls=%async_computation.4 | async-start | bytes 1081344 | tf_op jit(solution)/shard_map/all_gather | solution.py:80
  318.9 246.8 %all-gather.17.cloned.1.call-start = ((), (), s32[]{:S(2)}) async-start(), calls=%async_computation.5 | async-start | bytes 17825792 | tf_op jit(solution)/shard_map/all_gather | solution.py:85
Sparse Core Ops, SparseCore 0:
  10.1 69.4 all-gather.10
  83.5 64.6 all-gather.12
  152.9 99.2 reduce-scatter.1
  319.0 55.5 all-gather.14
  376.5 189.1 all-gather.16
where the time goes:
time: 655 us; the launch traced here: 654 us
  waiting for transfers between devices  477 us (73%)
  blocking collectives  134 us (20%)
  between operations  15.2 us (2%)
  matrix products  13.2 us (2%)
  other arithmetic  6.97 us (1%)
  local copies, waits for them, and re-layouts  6.76 us (1%)
    all_gather x1, waiting for transfers between devices, body(): lax.all_gather(head, 'dp', axis=1, tiled=True)  191 us
    reduce_scatter x1, waiting for transfers between devices, body(): lax.psum_scatter(partial_out, 'tensor', scatter_dimension=2, tiled=True)  98.6 us
    all_gather x3, blocking collectives, joined(): pieces = jax.tree.map(lambda part: lax.all_gather(part, axis), value)  70.1 us
    all_gather x1, waiting for transfers between devices, body(): everything = lax.all_gather(pages, 'dp', axis=1, tiled=True)  68.5 us
    all_gather x1, waiting for transfers between devices, body(): lax.all_gather(shifted, 'tensor', axis=2, tiled=True)  64.8 us
    psum x1, blocking collectives, body(): lax.psum((jnp.sum(residual, axis=-1), jnp.sum(residual * residual, axis=-...  64.3 us
    all_gather x1, waiting for transfers between devices, body(): normed = lax.all_gather(normed_local, 'tensor', axis=2, tiled=True)  53 us
  transfers between devices with their start and end apart: 5, of which 5 were waited for; matrix products, arithmetic and copies ran while one was open for 1% of the time, Pallas kernels for 0%

commit v1 on v0

--- a/solution.py
+++ b/solution.py
@@ -5,6 +5,28 @@
 
 D = 2048
 epsilon = 1e-05
+
+
+def in_order(tiles, dim):
+    shape = list(tiles.shape[1:])
+    shape[dim] *= tiles.shape[0]
+    return jnp.moveaxis(tiles, 0, dim).reshape(shape)
+
+
+def gather_around(x, axis, dim):
+    length = lax.axis_size(axis)
+    pairs = [(i, (i + 1) % length) for i in range(length)]
+    back = [(b, a) for a, b in pairs]
+    lower, upper = ([], [])
+    for step in range(length - 1):
+        if step % 2 == 0:
+            lower.append(lax.ppermute(lower[-1] if lower else x, axis, pairs))
+        else:
+            upper.append(lax.ppermute(upper[-1] if upper else x, axis, back))
+    pieces = jnp.stack([*lower[::-1], x, *upper])
+    shift = lax.axis_index(axis) - len(lower)
+    pieces = pieces[(jnp.arange(length) - shift) % length]
+    return in_order(pieces, dim)
 
 
 def joined(value, axis, join):
@@ -80,10 +102,7 @@
     normed = lax.all_gather(normed_local, "tensor", axis=2, tiled=True)
     vocab_local = head.shape[2]
     logits = jnp.einsum(
-        "msd,mdv->msv",
-        normed,
-        lax.all_gather(head, "dp", axis=1, tiled=True),
-        preferred_element_type=jnp.float32,
+        "msd,mdv->msv", normed, gather_around(head, "dp", 1), preferred_element_type=jnp.float32
     )
     peak = jnp.max(logits, axis=-1)
     totals = jnp.sum(jnp.exp(logits - peak[..., None]), axis=-1)

time: 655 us -> 475 us (0.73)
  waiting for transfers between devices: 477 us -> 179 us
  local copies, waits for them, and re-layouts: 6.76 us -> 68.3 us
  starting transfers between devices: 0.2 us -> 58 us
    all_gather x1 -> x0, waiting for transfers between devices: 191 us -> none  [body(): lax.all_gather(head, 'dp', axis=1, tiled=True)]
    ppermute x0 -> x15, waiting for transfers between devices: none -> 96.6 us  [the longest x8 96.5 us: gather_around(): lower.append(lax.ppermute(lower[-1] if lower else x, axis, pairs))]
    reduce_scatter x1, waiting for transfers between devices: 98.6 us -> 35 us  [body(): lax.psum_scatter(partial_out, 'tensor', scatter_dimension=2, tiled=True)]
    ppermute x0 -> x15, starting transfers between devices: none -> 57.8 us  [the longest x7 38.7 us: gather_around(): upper.append(lax.ppermute(upper[-1] if upper else x, axis, back))]
    all_gather x1, waiting for transfers between devices: 53 us -> 0.01 us  [body(): normed = lax.all_gather(normed_local, 'tensor', axis=2, tiled=True)]
    all_gather x1, waiting for transfers between devices: 64.8 us -> 15.2 us  [body(): lax.all_gather(shifted, 'tensor', axis=2, tiled=True)]
    all_gather x1, waiting for transfers between devices: 68.5 us -> 31 us  [body(): everything = lax.all_gather(pages, 'dp', axis=1, tiled=True)]
    unnamed x6 -> x21, local copies, waits for them, and re-layouts: 0.02 us -> 31.2 us
  transfers between devices with their start and end apart: 5 -> 19, of which waited for: 5 -> 8; matrix products, arithmetic and copies ran while one was open for 1% -> 16% of each run, Pallas kernels for 0% -> 0%
where the time goes in v1:
time: 475 us; the launch traced here: 473 us
  waiting for transfers between devices  179 us (38%)
  blocking collectives  132 us (28%)
  local copies, waits for them, and re-layouts  68.3 us (14%)
  starting transfers between devices  58 us (12%)
  between operations  15.4 us (3%)
  matrix products  13.1 us (3%)
  other arithmetic  7.63 us (2%)
    ppermute x8, waiting for transfers between devices, gather_around(): lower.append(lax.ppermute(lower[-1] if lower else x, axis, pairs))  96.5 us
    all_gather x3, blocking collectives, joined(): pieces = jax.tree.map(lambda part: lax.all_gather(part, axis), value)  67.8 us
    psum x1, blocking collectives, body(): lax.psum((jnp.sum(residual, axis=-1), jnp.sum(residual * residual, axis=-...  64.3 us
    ppermute x7, starting transfers between devices, gather_around(): upper.append(lax.ppermute(upper[-1] if upper else x, axis, back))  38.7 us
    reduce_scatter x1, waiting for transfers between devices, body(): lax.psum_scatter(partial_out, 'tensor', scatter_dimension=2, tiled=True)  35 us
    unnamed x21, local copies, waits for them, and re-layouts  31.2 us
    all_gather x1, waiting for transfers between devices, body(): everything = lax.all_gather(pages, 'dp', axis=1, tiled=True)  31 us
    ppermute x8, starting transfers between devices, gather_around(): lower.append(lax.ppermute(lower[-1] if lower else x, axis, pairs))  19.2 us
  transfers between devices with their start and end apart: 19, of which 8 were waited for; matrix products, arithmetic and copies ran while one was open for 16% of the time, Pallas kernels for 0%

profile of v1, /device:TPU:1, one launch (start us, length us, event | category | flops | bytes accessed | tf_op | source)
XLA Modules:
  0.0 473.5 jit_solution(10213361912767682947)
XLA Ops:
  8.0 4.5 collective-permute-start
  12.5 9.5 %collective-permute-start.8 = (bf16[2,128,2048]{2,1,0:T(8,128)(2,1)}, bf16[2,128,2048]{2,1,0:T(8,128)(2,1)}, u32[]{:S(2)}, u32[]{:S(2)}) collective-permute-start(bf16[2,128,2048]{2,1,0:T(8,128)(2,1)} %param.23), channel_id=1, source_target_pairs={{32,0},{64,32},{96,64},{128,96},{160,128},{192,160},{224,192},{256... | collective-permute-start | bytes 3145736 | tf_op jit(solution)/shard_map/ppermute | solution.py:25
  22.0 25.6 %collective-permute-done = bf16[2,128,2048]{2,1,0:T(8,128)(2,1)} collective-permute-done((bf16[2,128,2048]{2,1,0:T(8,128)(2,1)}, bf16[2,128,2048]{2,1,0:T(8,128)(2,1)}, u32[]{:S(2)}, u32[]{:S(2)}) %collective-permute-start) | collective-permute-done | bytes 1048608 | tf_op jit(solution)/shard_map/ppermute | solution.py:23
  47.6 1.9 collective-permute-start.1
  52.7 4.6 collective-permute-start.9
  57.3 31.0 %all-gather.10.cloned.1.call-done = bf16[2,64,64,64]{3,2,1,0:T(8,128)(2,1)} async-done(((bf16[2,4,64,64]{3,2,1,0:T(8,128)(2,1)}), bf16[2,64,64,64]{3,2,1,0:T(8,128)(2,1)}) %all-gather.10.cloned.1.call-update) | async-done | bytes 1048592 | tf_op jit(solution)/shard_map/all_gather | solution.py:70
  88.3 2.2 gather_fusion
  90.7 1.9 collective-permute-start.2
  92.6 1.4 add_convert_fusion.1
  94.1 18.2 %collective-permute-done.2 = bf16[2,128,2048]{2,1,0:T(8,128)(2,1)} collective-permute-done((bf16[2,128,2048]{2,1,0:T(8,128)(2,1)}, bf16[2,128,2048]{2,1,0:T(8,128)(2,1)}, u32[]{:S(2)}, u32[]{:S(2)}) %collective-permute-start.2) | collective-permute-done | bytes 1048608 | tf_op jit(solution)/shard_map/ppermute | solution.py:23
  112.3 1.9 collective-permute-start.3
  114.2 4.6 collective-permute-start.10
  118.8 15.1 %collective-permute-done.3 = bf16[2,128,2048]{2,1,0:T(8,128)(2,1)} collective-permute-done((bf16[2,128,2048]{2,1,0:T(8,128)(2,1)}, bf16[2,128,2048]{2,1,0:T(8,128)(2,1)}, u32[]{:S(2)}, u32[]{:S(2)}) %collective-permute-start.3) | collective-permute-done | bytes 1048608 | tf_op jit(solution)/shard_map/ppermute | solution.py:23
  133.9 1.9 collective-permute-start.4
  135.8 4.6 collective-permute-start.11
  140.4 15.2 %all-gather.12.cloned.1.call-done = bf16[2,128,2048]{1,2,0:T(8,128)(2,1)} async-done(((bf16[2,128,64]{1,2,0:T(8,128)(2,1)}), bf16[2,128,2048]{1,2,0:T(8,128)(2,1)}) %all-gather.12.cloned.1.call-update) | async-done | bytes 1048592 | tf_op jit(solution)/shard_map/all_gather | solution.py:81
  155.7 4.5 fusion.4
  160.3 3.2 collective-permute-start.5
  163.5 4.4 collective-permute-start.12
  167.9 18.3 %collective-permute-done.5 = bf16[2,128,2048]{2,1,0:T(8,128)(2,1)} collective-permute-done((bf16[2,128,2048]{2,1,0:T(8,128)(2,1)}, bf16[2,128,2048]{2,1,0:T(8,128)(2,1)}, u32[]{:S(2)}, u32[]{:S(2)}) %collective-permute-start.5) | collective-permute-done | bytes 1048608 | tf_op jit(solution)/shard_map/ppermute | solution.py:23
  186.2 1.9 collective-permute-start.6
  188.1 6.5 %collective-permute-start.13 = (bf16[2,128,2048]{2,1,0:T(8,128)(2,1)S(1)}, bf16[2,128,2048]{2,1,0:T(8,128)(2,1)S(1)}, u32[]{:S(2)}, u32[]{:S(2)}) collective-permute-start(bf16[2,128,2048]{2,1,0:T(8,128)(2,1)S(1)} %collective-permute-done.12), channel_id=1, source_target_pairs={{32,0},{64,32},{96,64},{128,96},{160,128},{192,160},{224,192},{256... | collective-permute-start | bytes 3145736 | tf_op jit(solution)/shard_map/ppermute | solution.py:25
  194.7 19.2 %collective-permute-done.6 = bf16[2,128,2048]{2,1,0:T(8,128)(2,1)} collective-permute-done((bf16[2,128,2048]{2,1,0:T(8,128)(2,1)}, bf16[2,128,2048]{2,1,0:T(8,128)(2,1)}, u32[]{:S(2)}, u32[]{:S(2)}) %collective-permute-start.6) | collective-permute-done | bytes 1048608 | tf_op jit(solution)/shard_map/ppermute | solution.py:23
  213.9 1.9 collective-permute-start.7
  220.0 4.6 collective-permute-start.14
  224.6 35.0 %reduce-scatter.2.cloned.1.call-done = f32[2,128,64]{1,2,0:T(8,128)} async-done(((f32[2,128,2048]{1,2,0:T(8,128)}), f32[2,128,64]{1,2,0:T(8,128)}) %reduce-scatter.2.cloned.1.call-update) | async-done | bytes 65552 | tf_op jit(solution)/shard_map/reduce_scatter | solution.py:87
  260.5 64.3 %all-reduce.1 = (f32[2,128]{1,0:T(2,128)S(1)}, f32[2,128]{1,0:T(2,128)S(1)}) all-reduce(f32[2,128]{1,0:T(2,128)S(1)} %get-tuple-element.47, f32[2,128]{1,0:T(2,128)S(1)} %get-tuple-element.46), channel_id=1, replica_groups=mesh['dp'=16,'tensor'=32] {'tensor'}, use_global_device_ids=true, to_apply=%region_4.5 | all-reduce | flops 512 | bytes 4096 | tf_op jit(solution)/shard_map/psum | solution.py:89
  324.8 1.6 add_convert_fusion
  326.4 2.3 bitcast_dynamic-update-slice_fusion.15
  328.7 2.3 bitcast_dynamic-update-slice_fusion.14
  331.0 2.3 bitcast_dynamic-update-slice_fusion.13
  333.3 2.3 bitcast_dynamic-update-slice_fusion.12
  335.7 2.3 bitcast_dynamic-update-slice_fusion.11
  338.0 2.3 bitcast_dynamic-update-slice_fusion.10
  340.3 2.3 bitcast_dynamic-update-slice_fusion.9
  342.6 2.3 bitcast_dynamic-update-slice_fusion.8
  346.1 2.3 bitcast_dynamic-update-slice_fusion.6
  348.4 2.3 bitcast_dynamic-update-slice_fusion.5
  350.7 2.3 bitcast_dynamic-update-slice_fusion.4
  353.0 2.4 bitcast_dynamic-update-slice_fusion.3
  357.6 2.3 bitcast_dynamic-update-slice_fusion
  359.9 13.1 %gather_fusion.1 = bf16[16,2,128,2048]{3,2,1,0:T(8,128)(2,1)} fusion(bf16[16,2,128,2048]{3,2,1,0:T(8,128)(2,1)} %bitcast_dynamic-update-slice_fusion, s32[1024]{0:T(1024)S(1)} %pad_clamp_fusion), kind=kCustom, calls=%fused_computation.1 | custom fusion | bytes 33554496 | tf_op jit(solution)/shard_map/gather | solution.py:28
  373.0 14.2 %copy.22 = bf16[2,16,128,2048]{3,2,1,0:T(8,128)(2,1)} copy(bf16[2,16,128,2048]{3,2,0,1:T(8,128)(2,1)} %bitcast.89) | data formatting | bytes 33554432 | tf_op jit(solution)/shard_map/transpose | solution.py:13
  387.2 8.6 %fusion.13 = (f32[2,128]{1,0:T(2,128)S(1)}, f32[2,128,2048]{2,1,0:T(8,128)S(1)}) fusion(bf16[2,128,2048]{1,2,0:T(8,128)(2,1)} %all-gather.14.cloned.1.call-done, bf16[2,2048,2048]{2,1,0:T(8,128)(2,1)} %bitcast.88), kind=kOutput, calls=%fused_computation.69 | convolution fusion | flops 2148007680 | bytes 19923968 | tf_op jit(solution)/shard_map/msd,mdv->msv/dot_general | solution.py:104
  396.6 21.3 %all-gather.5 = f32[32,2,128]{2,1,0:T(2,128)S(1)} all-gather(f32[1,2,128]{2,1,0:T(2,128)S(1)} %bitcast.94), channel_id=4, replica_groups=mesh['dp'=16,'tensor'=32] {'tensor'}, dimensions={0}, use_global_device_ids=true | all-gather | bytes 33792 | tf_op jit(solution)/shard_map/all_gather | solution.py:33
  417.9 25.1 %all-gather.4 = f32[32,2,128]{2,1,0:T(2,128)S(1)} all-gather(f32[1,2,128]{2,1,0:T(2,128)S(1)} %bitcast.93), channel_id=3, replica_groups=mesh['dp'=16,'tensor'=32] {'tensor'}, dimensions={0}, use_global_device_ids=true | all-gather | bytes 33792 | tf_op jit(solution)/shard_map/all_gather | solution.py:33
  443.0 21.4 %all-gather.3 = f32[32,2,128]{2,1,0:T(2,128)S(1)} all-gather(f32[1,2,128]{2,1,0:T(2,128)S(1)} %bitcast.92), channel_id=2, replica_groups=mesh['dp'=16,'tensor'=32] {'tensor'}, dimensions={0}, use_global_device_ids=true | all-gather | bytes 33792 | tf_op jit(solution)/shard_map/all_gather | solution.py:33
  464.4 1.3 while.14
  (90 shorter events, 14.2 us)
Async XLA Ops:
  7.2 148.5 %copy-start = (bf16[2,256,2048]{2,1,0:T(8,128)(2,1)S(1)}, bf16[2,256,2048]{2,1,0:T(8,128)(2,1)}, u32[]{:S(2)}) copy-start(bf16[2,256,2048]{2,1,0:T(8,128)(2,1)} %param.20) | copy-start | bytes 6291460
  7.2 337.8 %copy-start.2 = (bf16[2,128,2048]{2,1,0:T(8,128)(2,1)S(1)}, bf16[2,128,2048]{2,1,0:T(8,128)(2,1)}, u32[]{:S(2)}) copy-start(bf16[2,128,2048]{2,1,0:T(8,128)(2,1)} %param.23) | copy-start | bytes 3145732
  7.2 81.1 %all-gather.10.cloned.1.call-start = ((), (), s32[]{:S(2)}) async-start(), calls=%async_computation.1 | async-start | bytes 2228224 | tf_op jit(solution)/shard_map/all_gather | solution.py:70
  7.9 147.7 %all-gather.12.cloned.1.call-start = ((), (), s32[]{:S(2)}) async-start(), calls=%async_computation.2 | async-start | bytes 1081344 | tf_op jit(solution)/shard_map/all_gather | solution.py:81
  8.0 39.7 %collective-permute-start = (bf16[2,128,2048]{2,1,0:T(8,128)(2,1)}, bf16[2,128,2048]{2,1,0:T(8,128)(2,1)}, u32[]{:S(2)}, u32[]{:S(2)}) collective-permute-start(bf16[2,128,2048]{2,1,0:T(8,128)(2,1)} %param.23), channel_id=1, source_target_pairs={{0,32},{32,64},{64,96},{96,128},{128,160},{160,192},{192,224},{224... | collective-permute-start | bytes 3145736 | tf_op jit(solution)/shard_map/ppermute | solution.py:23
  12.5 40.2 %collective-permute-start.8 = (bf16[2,128,2048]{2,1,0:T(8,128)(2,1)}, bf16[2,128,2048]{2,1,0:T(8,128)(2,1)}, u32[]{:S(2)}, u32[]{:S(2)}) collective-permute-start(bf16[2,128,2048]{2,1,0:T(8,128)(2,1)} %param.23), channel_id=1, source_target_pairs={{32,0},{64,32},{96,64},{128,96},{160,128},{192,160},{224,192},{256... | collective-permute-start | bytes 3145736 | tf_op jit(solution)/shard_map/ppermute | solution.py:25
  47.6 43.0 %collective-permute-start.1 = (bf16[2,128,2048]{2,1,0:T(8,128)(2,1)}, bf16[2,128,2048]{2,1,0:T(8,128)(2,1)}, u32[]{:S(2)}, u32[]{:S(2)}) collective-permute-start(bf16[2,128,2048]{2,1,0:T(8,128)(2,1)} %collective-permute-done), channel_id=1, source_target_pairs={{0,32},{32,64},{64,96},{96,128},{128,160},{160,192},{192,224},{224... | collective-permute-start | bytes 3145736 | tf_op jit(solution)/shard_map/ppermute | solution.py:23
  52.7 61.5 %collective-permute-start.9 = (bf16[2,128,2048]{2,1,0:T(8,128)(2,1)}, bf16[2,128,2048]{2,1,0:T(8,128)(2,1)}, u32[]{:S(2)}, u32[]{:S(2)}) collective-permute-start(bf16[2,128,2048]{2,1,0:T(8,128)(2,1)} %collective-permute-done.8), channel_id=1, source_target_pairs={{32,0},{64,32},{96,64},{128,96},{160,128},{192,160},{224,192},{256... | collective-permute-start | bytes 3145736 | tf_op jit(solution)/shard_map/ppermute | solution.py:25
  90.7 21.6 %collective-permute-start.2 = (bf16[2,128,2048]{2,1,0:T(8,128)(2,1)}, bf16[2,128,2048]{2,1,0:T(8,128)(2,1)}, u32[]{:S(2)}, u32[]{:S(2)}) collective-permute-start(bf16[2,128,2048]{2,1,0:T(8,128)(2,1)} %collective-permute-done.1), channel_id=1, source_target_pairs={{0,32},{32,64},{64,96},{96,128},{128,160},{160,192},{192,224},{224... | collective-permute-start | bytes 3145736 | tf_op jit(solution)/shard_map/ppermute | solution.py:23
  94.0 165.6 %reduce-scatter.2.cloned.1.call-start = ((), (), s32[]{:S(2)}) async-start(), calls=%async_computation.3 | async-start | bytes 2162688 | tf_op jit(solution)/shard_map/reduce_scatter | solution.py:87
  112.3 21.6 %collective-permute-start.3 = (bf16[2,128,2048]{2,1,0:T(8,128)(2,1)}, bf16[2,128,2048]{2,1,0:T(8,128)(2,1)}, u32[]{:S(2)}, u32[]{:S(2)}) collective-permute-start(bf16[2,128,2048]{2,1,0:T(8,128)(2,1)} %collective-permute-done.2), channel_id=1, source_target_pairs={{0,32},{32,64},{64,96},{96,128},{128,160},{160,192},{192,224},{224... | collective-permute-start | bytes 3145736 | tf_op jit(solution)/shard_map/ppermute | solution.py:23
  114.2 21.6 %collective-permute-start.10 = (bf16[2,128,2048]{2,1,0:T(8,128)(2,1)}, bf16[2,128,2048]{2,1,0:T(8,128)(2,1)}, u32[]{:S(2)}, u32[]{:S(2)}) collective-permute-start(bf16[2,128,2048]{2,1,0:T(8,128)(2,1)} %collective-permute-done.9), channel_id=1, source_target_pairs={{32,0},{64,32},{96,64},{128,96},{160,128},{192,160},{224,192},{256... | collective-permute-start | bytes 3145736 | tf_op jit(solution)/shard_map/ppermute | solution.py:25
  133.9 26.3 %collective-permute-start.4 = (bf16[2,128,2048]{2,1,0:T(8,128)(2,1)}, bf16[2,128,2048]{2,1,0:T(8,128)(2,1)}, u32[]{:S(2)}, u32[]{:S(2)}) collective-permute-start(bf16[2,128,2048]{2,1,0:T(8,128)(2,1)} %collective-permute-done.3), channel_id=1, source_target_pairs={{0,32},{32,64},{64,96},{96,128},{128,160},{160,192},{192,224},{224... | collective-permute-start | bytes 3145736 | tf_op jit(solution)/shard_map/ppermute | solution.py:23
  135.8 27.6 %collective-permute-start.11 = (bf16[2,128,2048]{2,1,0:T(8,128)(2,1)}, bf16[2,128,2048]{2,1,0:T(8,128)(2,1)}, u32[]{:S(2)}, u32[]{:S(2)}) collective-permute-start(bf16[2,128,2048]{2,1,0:T(8,128)(2,1)} %collective-permute-done.10), channel_id=1, source_target_pairs={{32,0},{64,32},{96,64},{128,96},{160,128},{192,160},{224,192},{256... | collective-permute-start | bytes 3145736 | tf_op jit(solution)/shard_map/ppermute | solution.py:25
  160.2 227.0 %all-gather.14.cloned.1.call-start = ((), (), s32[]{:S(2)}) async-start(), calls=%async_computation.4 | async-start | bytes 1081344 | tf_op jit(solution)/shard_map/all_gather | solution.py:102
  160.3 25.9 %collective-permute-start.5 = (bf16[2,128,2048]{2,1,0:T(8,128)(2,1)}, bf16[2,128,2048]{2,1,0:T(8,128)(2,1)}, u32[]{:S(2)}, u32[]{:S(2)}) collective-permute-start(bf16[2,128,2048]{2,1,0:T(8,128)(2,1)} %collective-permute-done.4), channel_id=1, source_target_pairs={{0,32},{32,64},{64,96},{96,128},{128,160},{160,192},{192,224},{224... | collective-permute-start | bytes 3145736 | tf_op jit(solution)/shard_map/ppermute | solution.py:23
  163.5 24.7 %collective-permute-start.12 = (bf16[2,128,2048]{2,1,0:T(8,128)(2,1)}, bf16[2,128,2048]{2,1,0:T(8,128)(2,1)S(1)}, u32[]{:S(2)}, u32[]{:S(2)}) collective-permute-start(bf16[2,128,2048]{2,1,0:T(8,128)(2,1)} %collective-permute-done.11), channel_id=1, source_target_pairs={{32,0},{64,32},{96,64},{128,96},{160,128},{192,160},{224,192},{256... | collective-permute-start | bytes 3145736 | tf_op jit(solution)/shard_map/ppermute | solution.py:25
  186.2 27.7 %collective-permute-start.6 = (bf16[2,128,2048]{2,1,0:T(8,128)(2,1)}, bf16[2,128,2048]{2,1,0:T(8,128)(2,1)}, u32[]{:S(2)}, u32[]{:S(2)}) collective-permute-start(bf16[2,128,2048]{2,1,0:T(8,128)(2,1)} %collective-permute-done.5), channel_id=1, source_target_pairs={{0,32},{32,64},{64,96},{96,128},{128,160},{160,192},{192,224},{224... | collective-permute-start | bytes 3145736 | tf_op jit(solution)/shard_map/ppermute | solution.py:23
  188.1 31.9 %collective-permute-start.13 = (bf16[2,128,2048]{2,1,0:T(8,128)(2,1)S(1)}, bf16[2,128,2048]{2,1,0:T(8,128)(2,1)S(1)}, u32[]{:S(2)}, u32[]{:S(2)}) collective-permute-start(bf16[2,128,2048]{2,1,0:T(8,128)(2,1)S(1)} %collective-permute-done.12), channel_id=1, source_target_pairs={{32,0},{64,32},{96,64},{128,96},{160,128},{192,160},{224,192},{256... | collective-permute-start | bytes 3145736 | tf_op jit(solution)/shard_map/ppermute | solution.py:25
  213.9 112.5 %collective-permute-start.7 = (bf16[2,128,2048]{2,1,0:T(8,128)(2,1)}, bf16[2,128,2048]{2,1,0:T(8,128)(2,1)}, u32[]{:S(2)}, u32[]{:S(2)}) collective-permute-start(bf16[2,128,2048]{2,1,0:T(8,128)(2,1)} %collective-permute-done.6), channel_id=1, source_target_pairs={{0,32},{32,64},{64,96},{96,128},{128,160},{160,192},{192,224},{224... | collective-permute-start | bytes 3145736 | tf_op jit(solution)/shard_map/ppermute | solution.py:23
  220.0 137.6 %collective-permute-start.14 = (bf16[2,128,2048]{2,1,0:T(8,128)(2,1)S(1)}, bf16[2,128,2048]{2,1,0:T(8,128)(2,1)}, u32[]{:S(2)}, u32[]{:S(2)}) collective-permute-start(bf16[2,128,2048]{2,1,0:T(8,128)(2,1)S(1)} %collective-permute-done.13), channel_id=1, source_target_pairs={{32,0},{64,32},{96,64},{128,96},{160,128},{192,160},{224,192},{256... | collective-permute-start | bytes 3145736 | tf_op jit(solution)/shard_map/ppermute | solution.py:25
  373.0 94.0 %copy-start.1 = (bf16[2,256,2048]{2,1,0:T(8,128)(2,1)S(1)}, bf16[2,256,2048]{2,1,0:T(8,128)(2,1)}, u32[]{:S(2)}) copy-start(bf16[2,256,2048]{2,1,0:T(8,128)(2,1)} %param.20) | copy-start | bytes 6291460
Sparse Core Ops, SparseCore 0:
  10.1 78.1 all-gather.9
  94.1 61.4 all-gather.11
  160.3 99.2 reduce-scatter.1
  326.5 55.5 all-gather.13
